TPU v7x, 256 devices: a whole 4x4x8 slice. The times are simulated.
256 devices in a mesh: grp: 8 (over y, core), dom: 32 (over x, z).
Axes of the slice: x: 4, y: 4, z: 8, core: 2. Of those that a mesh axis runs over, the one named last changes fastest.
Arguments:
- fine_nodes: bfloat16 [8, 24576, 128], P('grp', 'dom'), may hold values from -6 to 6
- fine_edges: bfloat16 [8, 294912, 128], P('grp', 'dom'), may hold values from -6 to 6
- fine_senders: int32 [8, 294912], P('grp', 'dom'), may hold values from 0 to 1535
- fine_receivers: int32 [8, 294912], P('grp', 'dom'), may hold values from 0 to 767, as said below
- edge_count: int32 [8, 32], P('grp', 'dom'), may hold values from 4608 to 9216, as said below
- ghost_send: int32 [8, 1024, 24], P('grp', 'dom'), may hold values from 0 to 767
- fine_parent: int32 [8, 24576], P('grp', 'dom'), may hold values from 0 to 16383, as said below
- coarse_nodes: bfloat16 [16384, 128], P('dom'), may hold values from -6 to 6
- coarse_edges: bfloat16 [131072, 128], P('dom'), may hold values from -6 to 6
- coarse_senders: int32 [131072], P('dom'), may hold values from 0 to 16383
- coarse_receivers: int32 [131072], P('dom'), may hold values from 0 to 511, as said below
- edge_in: bfloat16 [2, 384, 128], replicated, may hold values from -0.3125 to 0.3125
- node_in: bfloat16 [3, 256, 128], replicated, may hold values from -0.375 to 0.375
- mlp_out: bfloat16 [5, 128, 128], replicated, may hold values from -0.5 to 0.5
Outputs:
- fine_out: bfloat16 [8, 24576, 128], P('grp', 'dom')
- coarse_out: bfloat16 [16384, 128], P('dom')
Inputs may be any that keep to these rules, and one draw needn't show every extreme that they name: `edge_count`: each device's live edge slot count; slots from that count on are padding; 9216 on at least one device. `fine_receivers`: nondecreasing along each device's 9216 slots; padding slots hold 767. `fine_senders`: below 768: a local node; 768 + s * 24 + k: ghost slot k received from dom index s of the same slab. `ghost_send`: local node indices; row p of a device's block lists the nodes sent to dom index p. `fine_parent`: global coarse index; owner o holds coarse nodes o * 512 to (o + 1) * 512 - 1. Most parents of a fine node of dom index d are owned by d itself; the others may be owned by any owner. `coarse_senders`: global coarse index of the sender. `coarse_receivers`: nondecreasing within each owner's 4096 edges.
All inputs are finite; a program needn't handle non-finite values.
Results may differ from a plain program's by a relative error of at most 0.015.
Values may be sent and summed in bfloat16 or wider, within the bound.
A program may use at most 64 MiB of HBM per device.

v0:
```python
import math
import jax
import jax.numpy as jnp
from jax import lax
from jax.sharding import Mesh
from jax.sharding import PartitionSpec as P

DOM = ("dom_0", "dom_1")


def in_blocks(array, dim, peers):
    shape = array.shape
    blocks = array.reshape(*shape[:dim], peers, shape[dim] // peers, *shape[dim + 1 :])
    return jnp.moveaxis(blocks, dim, 0)


def summed_on_arrival(array, axis, dim):
    peers = lax.axis_size(axis)
    blocks = lax.all_to_all(in_blocks(array, dim, peers), axis, 0, 0, tiled=True)
    return jnp.sum(blocks.astype(jnp.float32), axis=0)


def side_by_side(arrays, axis, dim, along):
    widths = [math.prod(a.shape[along:]) for a in arrays]
    both = jnp.concatenate(
        [a.reshape(*a.shape[:along], w) for a, w in zip(arrays, widths)], axis=along
    )
    out = summed_on_arrival(both, axis, dim)
    blocks = jnp.split(out, [sum(widths[:k]) for k in range(1, len(widths))], axis=along)
    return tuple((b.reshape(*out.shape[:along], *a.shape[along:]) for a, b in zip(arrays, blocks)))


def joined_along(blocks, dim):
    shape = list(blocks.shape[1:])
    shape[dim] *= blocks.shape[0]
    return jnp.moveaxis(blocks, 0, dim).reshape(shape)


def copy_for_each(array, axis):
    peers = lax.axis_size(axis)
    return lax.all_to_all(
        jnp.broadcast_to(array[None], (peers, *array.shape)), axis, 0, 0, tiled=True
    )


def gather_directly(array, axis, dim):
    return joined_along(copy_for_each(array, axis), dim)


def sent_together(arrays, axis, dim, along):
    widths = [math.prod(a.shape[along:]) for a in arrays]
    both = jnp.concatenate(
        [a.reshape(*a.shape[:along], w) for a, w in zip(arrays, widths)], axis=along
    )
    out = gather_directly(both, axis, dim)
    blocks = jnp.split(out, [sum(widths[:k]) for k in range(1, len(widths))], axis=along)
    return tuple((b.reshape(*out.shape[:along], *a.shape[along:]) for a, b in zip(arrays, blocks)))


def gather_in_order(array, axes, order):
    blocks = array[None]
    for k in order:
        blocks = lax.all_gather(blocks, axes[k], axis=0, tiled=True)
    current = [lax.axis_size(axes[k]) for k in reversed(order)]
    blocks = blocks.reshape(*current, *array.shape)
    turned = sorted(range(len(order)), key=lambda place: order[len(order) - 1 - place])
    return blocks.transpose(*turned, *range(len(order), blocks.ndim)).reshape(-1, *array.shape)


def whole_of(array, axes, order, dim):
    return joined_along(gather_in_order(array, axes, order), dim)


def layer_norm(values):
    centre = values - jnp.mean(values, -1, keepdims=True)
    spread = jnp.mean(centre * centre, -1, keepdims=True)
    return centre * lax.rsqrt(spread + 1e-05)


def perceptron(inputs, w_first, w_second):
    hidden = jax.nn.silu(jnp.dot(inputs, w_first, preferred_element_type=jnp.float32)).astype(
        jnp.bfloat16
    )
    return layer_norm(jnp.dot(hidden, w_second, preferred_element_type=jnp.float32))


def per_device(
    fine_nodes,
    fine_edges,
    fine_senders,
    fine_receivers,
    edge_count,
    ghost_send,
    fine_parent,
    coarse_nodes,
    coarse_edges,
    coarse_senders,
    coarse_receivers,
    edge_in,
    node_in,
    mlp_out,
):
    domains = lax.axis_size(DOM)
    groups = lax.axis_size("grp")
    local = fine_nodes[0]
    node_rows, width = local.shape
    owner_rows = coarse_nodes.shape[0]
    coarse_total = owner_rows * domains
    outgoing = local[ghost_send[0]]
    incoming = lax.all_to_all(outgoing, DOM, split_axis=0, concat_axis=0, tiled=True)
    table = jnp.concatenate([local, incoming.reshape(-1, width)], 0)
    edges = fine_edges[0]
    receivers = fine_receivers[0]
    inputs = jnp.concatenate([edges, local[receivers], table[fine_senders[0]]], -1)
    edge_new = edges.astype(jnp.float32) + perceptron(inputs, edge_in[0], mlp_out[0])
    live = (jnp.arange(edges.shape[0]) < edge_count[0, 0]).astype(jnp.float32)
    summed = jax.ops.segment_sum(
        edge_new * live[:, None], receivers, num_segments=node_rows
    ).astype(jnp.bfloat16)
    fine_mid = (
        local.astype(jnp.float32)
        + perceptron(jnp.concatenate([local, summed], -1), node_in[0], mlp_out[1])
    ).astype(jnp.bfloat16)
    parents = fine_parent[0]
    ones_rows = jnp.ones(parents.shape, jnp.float32)
    mid_wide = fine_mid.astype(jnp.float32)
    piece = owner_rows // groups
    owner = parents // owner_rows
    within = parents % owner_rows
    mapped = within // piece * (domains * piece) + owner * piece + within % piece
    pooled = jax.ops.segment_sum(mid_wide, mapped, num_segments=coarse_total).reshape(
        groups, domains, piece, width
    )
    children = jax.ops.segment_sum(ones_rows, mapped, num_segments=coarse_total).reshape(
        groups, domains, piece
    )
    pooled, children = (
        lax.psum_scatter(
            pooled.astype(jnp.bfloat16), "grp", scatter_dimension=0, tiled=True
        ).astype(jnp.float32),
        lax.psum_scatter(
            children.astype(jnp.bfloat16), "grp", scatter_dimension=0, tiled=True
        ).astype(jnp.float32),
    )
    pooled, children = side_by_side(
        (pooled.astype(jnp.bfloat16), children.astype(jnp.bfloat16)), DOM, 1, 3
    )
    pooled, children = sent_together((pooled, children), "grp", 0, 3)
    pooled = pooled.reshape(owner_rows, width)
    children = children.reshape(owner_rows)
    coarse_mid = ((coarse_nodes.astype(jnp.float32) + pooled) / (1.0 + children)[:, None]).astype(
        jnp.bfloat16
    )
    coarse_table = whole_of(coarse_mid, DOM, (0, 1), 0)
    cinputs = jnp.concatenate(
        [coarse_edges, coarse_mid[coarse_receivers], coarse_table[coarse_senders]], -1
    )
    cedge_new = coarse_edges.astype(jnp.float32) + perceptron(cinputs, edge_in[1], mlp_out[2])
    csummed = jax.ops.segment_sum(cedge_new, coarse_receivers, num_segments=owner_rows).astype(
        jnp.bfloat16
    )
    coarse_out = (
        coarse_mid.astype(jnp.float32)
        + perceptron(jnp.concatenate([coarse_mid, csummed], -1), node_in[1], mlp_out[3])
    ).astype(jnp.bfloat16)
    updated_table = whole_of(coarse_out, DOM, (0, 1), 0)
    above = updated_table[parents]
    fine_out = (
        mid_wide + perceptron(jnp.concatenate([fine_mid, above], -1), node_in[2], mlp_out[4])
    ).astype(jnp.bfloat16)
    return (fine_out[None], coarse_out)


def solution(mesh):
    torus = Mesh(mesh.devices.reshape(mesh.shape["grp"], 4, 8), ("grp", "dom_0", "dom_1"))
    in_specs = (
        P("grp", DOM, None),
        P("grp", DOM, None),
        P("grp", DOM),
        P("grp", DOM),
        P("grp", DOM),
        P("grp", DOM, None),
        P("grp", DOM),
        P(DOM, None),
        P(DOM, None),
        P(DOM),
        P(DOM),
        P(),
        P(),
        P(),
    )
    out_specs = (P("grp", DOM, None), P(DOM, None))
    return jax.shard_map(
        per_device, mesh=torus, in_specs=in_specs, out_specs=out_specs, check_vma=False
    )
```

profile of v0, /device:TPU:1, one launch (start us, length us, event | category | flops | bytes accessed | tf_op | source)
XLA Modules:
  0.0 494.9 jit_solution(16880242438352926247)
XLA Ops:
  8.1 3.2 gather_fusion.1
  11.4 11.9 %all-to-all-start = ((bf16[32,24,128]{2,1,0:T(8,128)(2,1)}), bf16[32,24,128]{2,1,0:T(8,128)(2,1)S(1)}, u32[]{:S(2)}, u32[]{:S(2)}) async-start(bf16[32,24,128]{2,1,0:T(8,128)(2,1)} %bitcast.8), calls=%async_computation | async-start | bytes 393216 | tf_op jit(solution)/shard_map/all_to_all | solution.py:110
  24.0 4.6 scatter_custom_fusion.2
  32.2 27.0 %gather_fusion = bf16[9216,128]{1,0:T(8,128)(2,1)S(1)} fusion(bf16[768,128]{1,0:T(8,128)(2,1)S(1)} %bitcast.111, s32[9216]{0:T(1024)S(1)} %broadcast_clamp_fusion.1), kind=kCustom, calls=%fused_computation | custom fusion | bytes 4755456 | tf_op jit(solution)/shard_map/gather | solution.py:114
  59.2 2.5 copy.87
  61.7 4.3 copy.81
  67.1 27.0 %gather_fusion.2 = bf16[9216,128]{1,0:T(8,128)(2,1)S(1)} fusion(bf16[1536,128]{1,0:T(8,128)(2,1)S(1)} %copy.86, s32[9216]{0:T(1024)S(1)} %broadcast_clamp_fusion), kind=kCustom, calls=%fused_computation.2 | custom fusion | bytes 4755456 | tf_op jit(solution)/shard_map/gather | solution.py:114
  94.1 2.5 copy.88
  96.6 6.8 %fusion.114 = (f32[9216]{0:T(1024)S(1)}, f32[9216,128]{0,1:T(8,128)}) fusion(bf16[5,128,128]{2,1,0:T(8,128)(2,1)} %param.27, bf16[9216,128]{0,1:T(8,128)(2,1)} %copy.88, bf16[9216,128]{0,1:T(8,128)(2,1)} %copy.87, bf16[9216,128]{0,1:T(8,128)(2,1)} %bitcast.114, bf16[2,384,128]{2,1,0:T(8,128)(2,1)S(1)} %copy-done.7), kind=kOutput, calls=%fused_computation.141 | convolution fusion | flops 1236261888 | bytes 11964416 | tf_op jit(solution)/shard_map/dot_general | solution.py:84
  103.4 3.0 multiply_reduce_fusion
  107.2 3.0 add_multiply_fusion
  110.2 6.1 %copy.89 = f32[9216,128]{1,0:T(8,128)} copy(f32[9216,128]{0,1:T(8,128)} %add_multiply_fusion) | data formatting | bytes 9437184 | tf_op jit(solution)/shard_map/mul | solution.py:118
  116.3 61.0 %scatter_custom_fusion = f32[768,128]{1,0:T(8,128)S(1)} fusion(s32[9216]{0:T(1024)} %bitcast.128, f32[9216,128]{1,0:T(8,128)} %copy.89, f32[]{:T(128)} %constant.85.clone.1), kind=kCustom, calls=%fused_computation.68 | custom fusion | flops 1179648 | bytes 393728 | tf_op jit(solution)/shard_map/scatter-add | solution.py:117
  179.0 9.7 %scatter_custom_fusion.1 = f32[16384,128]{1,0:T(8,128)} fusion(s32[768]{0:T(1024)S(1)} %get-tuple-element.11, f32[768,128]{1,0:T(8,128)S(1)} %copy.92, f32[]{:T(128)} %constant.85.clone.1), kind=kCustom, calls=%fused_computation.19 | custom fusion | flops 98304 | bytes 8388612 | tf_op jit(solution)/shard_map/scatter-add | solution.py:131
  188.8 5.1 %convert_element_type.86 = bf16[16384,128]{1,0:T(8,128)(2,1)} convert(f32[16384,128]{1,0:T(8,128)} %scatter_custom_fusion.1) | non-fusion elementwise | flops 2097152 | bytes 12582912 | tf_op jit(solution)/shard_map/convert_element_type | solution.py:139
  195.0 38.6 %reduce-scatter.3.cloned.1.call-done = bf16[1,32,64,128]{3,2,1,0:T(8,128)(2,1)} async-done(((bf16[8,32,64,128]{3,2,1,0:T(8,128)(2,1)}), bf16[1,32,64,128]{3,2,1,0:T(8,128)(2,1)}) %reduce-scatter.3.cloned.1.call-update) | async-done | bytes 524304 | tf_op jit(solution)/shard_map/reduce_scatter | solution.py:138
  234.9 30.8 %all_to_all.15 = bf16[32,1,1,64,129]{4,3,2,1,0:T(8,128)(2,1)S(1)} all-to-all(bf16[32,1,1,64,129]{4,3,2,1,0:T(8,128)(2,1)S(1)} %maximum_bitcast_fusion), channel_id=1, replica_groups=mesh['grp'=8,'dom_0'=4,'dom_1'=8] {'dom_0','dom_1'}, dimensions={0} | all-to-all | bytes 1056768 | tf_op jit(solution)/shard_map/all_to_all | solution.py:19
  266.7 12.0 %all-to-all-start.2 = ((f32[8,1,1,64,129]{4,3,2,1,0:T(8,128)}), f32[8,1,1,64,129]{4,3,2,1,0:T(8,128)S(1)}, u32[]{:S(2)}, u32[]{:S(2)}) async-start(f32[8,1,1,64,129]{4,3,2,1,0:T(8,128)} %broadcast_in_dim.28), calls=%async_computation.4 | async-start | bytes 1048576 | tf_op jit(solution)/shard_map/all_to_all | solution.py:41
  278.9 9.2 %all-to-all-done.2 = f32[8,1,1,64,129]{4,3,2,1,0:T(8,128)S(1)} async-done(((f32[8,1,1,64,129]{4,3,2,1,0:T(8,128)}), f32[8,1,1,64,129]{4,3,2,1,0:T(8,128)S(1)}, u32[]{:S(2)}, u32[]{:S(2)}) %all-to-all-start.2) | async-done | bytes 264224 | tf_op jit(solution)/shard_map/all_to_all | solution.py:41
  288.5 9.9 %all-gather = bf16[2048,128]{0,1:T(8,128)(2,1)S(1)} all-gather(bf16[512,128]{0,1:T(8,128)(2,1)S(1)} %divide_convert_fusion), channel_id=2, replica_groups=mesh['grp'=8,'dom_0'=4,'dom_1'=8] {'dom_0'}, dimensions={0}, use_global_device_ids=true | all-gather | bytes 655360 | tf_op jit(solution)/shard_map/all_gather | solution.py:63
  300.4 14.9 %gather_fusion.3 = bf16[4096,128]{1,0:T(8,128)(2,1)} fusion(bf16[512,128]{1,0:T(8,128)(2,1)S(1)} %copy.96, s32[4096]{0:T(1024)S(1)} %fusion.94), kind=kCustom, calls=%fused_computation.3 | custom fusion | bytes 2113536 | tf_op jit(solution)/shard_map/gather | solution.py:156
  315.3 37.2 %all-gather.5.cloned.1.call-done = bf16[32,512,128]{2,1,0:T(8,128)(2,1)} async-done(((bf16[4,512,128]{2,1,0:T(8,128)(2,1)}), bf16[32,512,128]{2,1,0:T(8,128)(2,1)}) %all-gather.5.cloned.1.call-update) | async-done | bytes 4194320 | tf_op jit(solution)/shard_map/all_gather | solution.py:63
  352.5 4.6 copy.98
  357.1 17.0 %gather_fusion.4 = bf16[4096,128]{1,0:T(8,128)(2,1)} fusion(bf16[16384,128]{1,0:T(8,128)(2,1)} %bitcast.112, s32[4096]{0:T(1024)S(1)} %fusion.95), kind=kCustom, calls=%fused_computation.4 | custom fusion | bytes 2113536 | tf_op jit(solution)/shard_map/gather | solution.py:156
  374.1 3.3 fusion.124
  377.7 1.7 multiply_add_fusion
  379.4 1.9 copy.99
  381.3 26.5 %scatter_custom_fusion.3 = f32[512,128]{1,0:T(8,128)S(1)} fusion(s32[4096]{0:T(1024)S(1)} %copy-done.6, f32[4096,128]{1,0:T(8,128)S(1)} %copy.99, f32[]{:T(128)} %constant.85.clone.1), kind=kCustom, calls=%fused_computation.71 | custom fusion | flops 524288 | bytes 262148 | tf_op jit(solution)/shard_map/scatter-add | solution.py:159
  409.3 11.7 %all-gather.1 = bf16[2048,128]{0,1:T(8,128)(2,1)S(1)} all-gather(bf16[512,128]{0,1:T(8,128)(2,1)S(1)} %add_convert_fusion.2), channel_id=3, replica_groups=mesh['grp'=8,'dom_0'=4,'dom_1'=8] {'dom_0'}, dimensions={0}, use_global_device_ids=true | all-gather | bytes 655360 | tf_op jit(solution)/shard_map/all_gather | solution.py:63
  422.7 54.3 %all-gather.7.cloned.1.call-done = bf16[32,512,128]{2,1,0:T(8,128)(2,1)} async-done(((bf16[4,512,128]{2,1,0:T(8,128)(2,1)}), bf16[32,512,128]{2,1,0:T(8,128)(2,1)}) %all-gather.7.cloned.1.call-update) | async-done | bytes 4194320 | tf_op jit(solution)/shard_map/all_gather | solution.py:63
  477.0 4.6 copy.102
  481.6 4.3 gather_fusion.5
  (88 shorter events, 19.8 us)
Async XLA Ops:
  7.2 25.0 %copy-start = (bf16[1,768,128]{2,1,0:T(8,128)(2,1)S(1)}, bf16[1,768,128]{2,1,0:T(8,128)(2,1)}, u32[]{:S(2)}) copy-start(bf16[1,768,128]{2,1,0:T(8,128)(2,1)} %param.14) | copy-start | bytes 589828
  11.4 55.3 %all-to-all-start = ((bf16[32,24,128]{2,1,0:T(8,128)(2,1)}), bf16[32,24,128]{2,1,0:T(8,128)(2,1)S(1)}, u32[]{:S(2)}, u32[]{:S(2)}) async-start(bf16[32,24,128]{2,1,0:T(8,128)(2,1)} %bitcast.8), calls=%async_computation | async-start | bytes 393216 | tf_op jit(solution)/shard_map/all_to_all | solution.py:110
  23.2 170.7 %reduce-scatter.5.cloned.1.call-start = ((), (), s32[]{:S(2)}) async-start(), calls=%async_computation.6 | async-start | bytes 73728 | tf_op jit(solution)/shard_map/reduce_scatter | solution.py:141
  29.4 204.2 %reduce-scatter.3.cloned.1.call-start = ((), (), s32[]{:S(2)}) async-start(), calls=%async_computation.5 | async-start | bytes 4718592 | tf_op jit(solution)/shard_map/reduce_scatter | solution.py:138
  94.1 2.5 copy-start.7
  96.6 9.8 %copy-start.2 = (bf16[1,9216,128]{1,2,0:T(8,128)(2,1)S(1)}, bf16[1,9216,128]{1,2,0:T(8,128)(2,1)}, u32[]{:S(2)}) copy-start(bf16[1,9216,128]{1,2,0:T(8,128)(2,1)} %copy.81) | copy-start | bytes 7077892
  103.4 3.8 copy-start.1
  195.0 83.8 %copy-start.4 = (bf16[512,128]{1,0:T(8,128)(2,1)S(1)}, bf16[512,128]{1,0:T(8,128)(2,1)}, u32[]{:S(2)}) copy-start(bf16[512,128]{1,0:T(8,128)(2,1)} %param.21) | copy-start | bytes 393220
  265.8 33.9 %copy-start.3 = (bf16[4096,128]{1,0:T(8,128)(2,1)S(1)}, bf16[4096,128]{1,0:T(8,128)(2,1)}, u32[]{:S(2)}) copy-start(bf16[4096,128]{1,0:T(8,128)(2,1)} %param.22) | copy-start | bytes 3145732
  266.7 21.4 %all-to-all-start.2 = ((f32[8,1,1,64,129]{4,3,2,1,0:T(8,128)}), f32[8,1,1,64,129]{4,3,2,1,0:T(8,128)S(1)}, u32[]{:S(2)}, u32[]{:S(2)}) async-start(f32[8,1,1,64,129]{4,3,2,1,0:T(8,128)} %broadcast_in_dim.28), calls=%async_computation.4 | async-start | bytes 1048576 | tf_op jit(solution)/shard_map/all_to_all | solution.py:41
  278.7 73.8 %all-gather.5.cloned.1.call-start = ((), (), s32[]{:S(2)}) async-start(), calls=%async_computation.7 | async-start | bytes 4718592 | tf_op jit(solution)/shard_map/all_gather | solution.py:63
  278.8 21.4 %copy-start.5 = (s32[4096]{0:T(1024)S(1)}, s32[4096]{0:T(1024)}, u32[]{:S(2)}) copy-start(s32[4096]{0:T(1024)} %param.23) | copy-start | bytes 49156
  278.9 21.4 %copy-start.6 = (s32[4096]{0:T(1024)S(1)}, s32[4096]{0:T(1024)}, u32[]{:S(2)}) copy-start(s32[4096]{0:T(1024)} %param.24) | copy-start | bytes 49156
  299.4 177.6 %all-gather.7.cloned.1.call-start = ((), (), s32[]{:S(2)}) async-start(), calls=%async_computation.8 | async-start | bytes 4718592 | tf_op jit(solution)/shard_map/all_gather | solution.py:63
  379.4 28.5 %copy-start.8 = (bf16[3,256,128]{2,1,0:T(8,128)(2,1)S(1)}, bf16[3,256,128]{2,1,0:T(8,128)(2,1)}, u32[]{:S(2)}) copy-start(bf16[3,256,128]{2,1,0:T(8,128)(2,1)} %param.26) | copy-start | bytes 589828
Sparse Core Ops, SparseCore 0:
  29.5 32.7 reduce-scatter.4
  194.0 39.5 reduce-scatter.2
  299.5 52.9 all-gather.4
  422.1 54.8 all-gather.6
where the time goes:
time: 496 us; the launch traced here: 495 us
  waiting for transfers between devices  139 us (28%)
  local copies, waits for them, and re-layouts  130 us (26%)
  other arithmetic  120 us (24%)
  blocking collectives  52.3 us (11%)
  starting transfers between devices  24.2 us (5%)
  between operations  14.9 us (3%)
  matrix products  14 us (3%)
    all_gather x2, waiting for transfers between devices, gather_in_order(): blocks = lax.all_gather(blocks, axes[k], axis=0, tiled=True)  91.5 us
    scatter-add x1, other arithmetic, per_device(): jax.ops.segment_sum(edge_new * live[:, None], receivers, num_segments=nod...  61 us
    reduce_scatter x1, waiting for transfers between devices, per_device(): lax.psum_scatter(pooled.astype(jnp.bfloat16), 'grp', scatter_dimension=0,...  38.6 us
    all_to_all x1, blocking collectives, summed_on_arrival(): lax.all_to_all(in_blocks(array, dim, peers), axis, 0, 0, tiled=True)  30.8 us
    gather x2, local copies, waits for them, and re-layouts, per_device(): local[receivers]  29.5 us
    gather x2, local copies, waits for them, and re-layouts, per_device(): table[fine_senders[0]]  29.5 us
    scatter-add x1, other arithmetic, per_device(): jax.ops.segment_sum(cedge_new, coarse_receivers, num_segments=owner_rows)  26.5 us
    all_gather x2, blocking collectives, gather_in_order(): blocks = lax.all_gather(blocks, axes[k], axis=0, tiled=True)  21.6 us
  transfers between devices with their start and end apart: 6, of which 4 were waited for; matrix products, arithmetic and copies ran while one was open for 38% of the time, Pallas kernels for 0%

commit v1 on v0

--- a/solution.py
+++ b/solution.py
@@ -60,7 +60,9 @@
 def gather_in_order(array, axes, order):
     blocks = array[None]
     for k in order:
-        blocks = lax.all_gather(blocks, axes[k], axis=0, tiled=True)
+        blocks = jnp.concatenate(
+            lax.all_to_all(jnp.stack([blocks] * lax.axis_size(axes[k])), axes[k], 0, 0), axis=0
+        )
     current = [lax.axis_size(axes[k]) for k in reversed(order)]
     blocks = blocks.reshape(*current, *array.shape)
     turned = sorted(range(len(order)), key=lambda place: order[len(order) - 1 - place])

time: 496 us -> 593 us (1.20)
  waiting for transfers between devices: 139 us -> 221 us
  starting transfers between devices: 24.2 us -> 37 us
    all_to_all x0 -> x2, waiting for transfers between devices: none -> 173 us  [gather_in_order(): lax.all_to_all(jnp.stack([blocks] * lax.axis_size(axes[k])), axes[k], 0, 0)]
    all_gather x2 -> x0, waiting for transfers between devices: 91.5 us -> none  [gather_in_order(): blocks = lax.all_gather(blocks, axes[k], axis=0, tiled=True)]
    all_gather x2 -> x0, blocking collectives: 21.6 us -> none  [gather_in_order(): blocks = lax.all_gather(blocks, axes[k], axis=0, tiled=True)]
    all_to_all x0 -> x2, blocking collectives: none -> 20.3 us  [gather_in_order(): lax.all_to_all(jnp.stack([blocks] * lax.axis_size(axes[k])), axes[k], 0, 0)]
    all_to_all x0 -> x2, starting transfers between devices: none -> 13 us  [gather_in_order(): lax.all_to_all(jnp.stack([blocks] * lax.axis_size(axes[k])), axes[k], 0, 0)]
    transpose x0 -> x2, local copies, waits for them, and re-layouts: none -> 9.22 us  [gather_in_order(): blocks.transpose(*turned, *range(len(order), blocks.ndim))]
    reshape x2 -> x0, local copies, waits for them, and re-layouts: 9.22 us -> none  [gather_in_order(): blocks = blocks.reshape(*current, *array.shape)]
    another operation x0 -> x4, local copies, waits for them, and re-layouts: none -> 6.06 us  [gather_in_order(): jnp.stack([blocks] * lax.axis_size(axes[k]))]
  transfers between devices with their start and end apart: 6 -> 6, of which waited for: 4 -> 4; matrix products, arithmetic and copies ran while one was open for 38% -> 31% of each run, Pallas kernels for 0% -> 0%
where the time goes in v1:
time: 593 us; the launch traced here: 592 us
  waiting for transfers between devices  221 us (37%)
  local copies, waits for them, and re-layouts  133 us (22%)
  other arithmetic  120 us (20%)
  blocking collectives  51.1 us (9%)
  starting transfers between devices  37 us (6%)
  between operations  15.2 us (3%)
  matrix products  13.9 us (2%)
    all_to_all x2, waiting for transfers between devices, gather_in_order(): lax.all_to_all(jnp.stack([blocks] * lax.axis_size(axes[k])), axes[k], 0, 0)  173 us
    scatter-add x1, other arithmetic, per_device(): jax.ops.segment_sum(edge_new * live[:, None], receivers, num_segments=nod...  61 us
    reduce_scatter x1, waiting for transfers between devices, per_device(): lax.psum_scatter(pooled.astype(jnp.bfloat16), 'grp', scatter_dimension=0,...  38.6 us
    all_to_all x1, blocking collectives, summed_on_arrival(): lax.all_to_all(in_blocks(array, dim, peers), axis, 0, 0, tiled=True)  30.8 us
    gather x2, local copies, waits for them, and re-layouts, per_device(): local[receivers]  29.5 us
    gather x2, local copies, waits for them, and re-layouts, per_device(): table[fine_senders[0]]  29.5 us
    scatter-add x1, other arithmetic, per_device(): jax.ops.segment_sum(cedge_new, coarse_receivers, num_segments=owner_rows)  26.5 us
    all_to_all x2, blocking collectives, gather_in_order(): lax.all_to_all(jnp.stack([blocks] * lax.axis_size(axes[k])), axes[k], 0, 0)  20.3 us
  transfers between devices with their start and end apart: 6, of which 4 were waited for; matrix products, arithmetic and copies ran while one was open for 31% of the time, Pallas kernels for 0%

profile of v1, /device:TPU:1, one launch (start us, length us, event | category | flops | bytes accessed | tf_op | source)
XLA Modules:
  0.0 591.9 jit_solution(11980014177610118631)
XLA Ops:
  8.1 3.2 gather_fusion.1
  11.4 11.9 %all-to-all-start = ((bf16[32,24,128]{2,1,0:T(8,128)(2,1)}), bf16[32,24,128]{2,1,0:T(8,128)(2,1)S(1)}, u32[]{:S(2)}, u32[]{:S(2)}) async-start(bf16[32,24,128]{2,1,0:T(8,128)(2,1)} %bitcast.8), calls=%async_computation | async-start | bytes 393216 | tf_op jit(solution)/shard_map/all_to_all | solution.py:112
  24.0 4.6 scatter_custom_fusion.2
  32.2 27.0 %gather_fusion = bf16[9216,128]{1,0:T(8,128)(2,1)S(1)} fusion(bf16[768,128]{1,0:T(8,128)(2,1)S(1)} %bitcast.107, s32[9216]{0:T(1024)S(1)} %broadcast_clamp_fusion.1), kind=kCustom, calls=%fused_computation | custom fusion | bytes 4755456 | tf_op jit(solution)/shard_map/gather | solution.py:116
  61.7 4.3 copy.81
  67.1 27.0 %gather_fusion.2 = bf16[9216,128]{1,0:T(8,128)(2,1)S(1)} fusion(bf16[1536,128]{1,0:T(8,128)(2,1)S(1)} %copy.86, s32[9216]{0:T(1024)S(1)} %broadcast_clamp_fusion), kind=kCustom, calls=%fused_computation.2 | custom fusion | bytes 4755456 | tf_op jit(solution)/shard_map/gather | solution.py:116
  96.6 6.8 %fusion.114 = (f32[9216]{0:T(1024)S(1)}, f32[9216,128]{0,1:T(8,128)}) fusion(bf16[5,128,128]{2,1,0:T(8,128)(2,1)} %param.27, bf16[9216,128]{0,1:T(8,128)(2,1)} %copy.88, bf16[9216,128]{0,1:T(8,128)(2,1)} %copy.87, bf16[9216,128]{0,1:T(8,128)(2,1)} %bitcast.110, bf16[2,384,128]{2,1,0:T(8,128)(2,1)S(1)} %copy-done.8), kind=kOutput, calls=%fused_computation.141 | convolution fusion | flops 1236261888 | bytes 11964416 | tf_op jit(solution)/shard_map/dot_general | solution.py:86
  103.4 3.0 multiply_reduce_fusion
  107.2 3.0 add_multiply_fusion
  110.2 6.1 %copy.89 = f32[9216,128]{1,0:T(8,128)} copy(f32[9216,128]{0,1:T(8,128)} %add_multiply_fusion) | data formatting | bytes 9437184 | tf_op jit(solution)/shard_map/mul | solution.py:120
  116.3 61.0 %scatter_custom_fusion = f32[768,128]{1,0:T(8,128)S(1)} fusion(s32[9216]{0:T(1024)} %bitcast.122, f32[9216,128]{1,0:T(8,128)} %copy.89, f32[]{:T(128)} %constant.85.clone.1), kind=kCustom, calls=%fused_computation.68 | custom fusion | flops 1179648 | bytes 393728 | tf_op jit(solution)/shard_map/scatter-add | solution.py:119
  179.0 9.7 %scatter_custom_fusion.1 = f32[16384,128]{1,0:T(8,128)} fusion(s32[768]{0:T(1024)S(1)} %get-tuple-element.11, f32[768,128]{1,0:T(8,128)S(1)} %copy.92, f32[]{:T(128)} %constant.85.clone.1), kind=kCustom, calls=%fused_computation.19 | custom fusion | flops 98304 | bytes 8388612 | tf_op jit(solution)/shard_map/scatter-add | solution.py:133
  188.8 5.1 convert_element_type.86
  195.0 38.6 %reduce-scatter.3.cloned.1.call-done = bf16[1,32,64,128]{3,2,1,0:T(8,128)(2,1)} async-done(((bf16[8,32,64,128]{3,2,1,0:T(8,128)(2,1)}), bf16[1,32,64,128]{3,2,1,0:T(8,128)(2,1)}) %reduce-scatter.3.cloned.1.call-update) | async-done | bytes 524304 | tf_op jit(solution)/shard_map/reduce_scatter | solution.py:140
  234.9 30.8 %all_to_all.35 = bf16[32,1,1,64,129]{4,3,2,1,0:T(8,128)(2,1)S(1)} all-to-all(bf16[32,1,1,64,129]{4,3,2,1,0:T(8,128)(2,1)S(1)} %maximum_bitcast_fusion), channel_id=1, replica_groups=mesh['grp'=8,'dom_0'=4,'dom_1'=8] {'dom_0','dom_1'}, dimensions={0} | all-to-all | bytes 1056768 | tf_op jit(solution)/shard_map/all_to_all | solution.py:19
  266.7 12.0 %all-to-all-start.2 = ((f32[8,1,1,64,129]{4,3,2,1,0:T(8,128)}), f32[8,1,1,64,129]{4,3,2,1,0:T(8,128)S(1)}, u32[]{:S(2)}, u32[]{:S(2)}) async-start(f32[8,1,1,64,129]{4,3,2,1,0:T(8,128)} %broadcast_in_dim.24), calls=%async_computation.4 | async-start | bytes 1048576 | tf_op jit(solution)/shard_map/all_to_all | solution.py:41
  278.8 9.2 %all-to-all-done.2 = f32[8,1,1,64,129]{4,3,2,1,0:T(8,128)S(1)} async-done(((f32[8,1,1,64,129]{4,3,2,1,0:T(8,128)}), f32[8,1,1,64,129]{4,3,2,1,0:T(8,128)S(1)}, u32[]{:S(2)}, u32[]{:S(2)}) %all-to-all-start.2) | async-done | bytes 264224 | tf_op jit(solution)/shard_map/all_to_all | solution.py:41
  288.7 11.0 %all_to_all.36 = bf16[4,1,512,128]{3,2,1,0:T(8,128)(2,1)S(1)} all-to-all(bf16[4,1,512,128]{3,2,1,0:T(8,128)(2,1)S(1)} %stack.12), channel_id=1, replica_groups=mesh['grp'=8,'dom_0'=4,'dom_1'=8] {'dom_0'}, dimensions={0} | all-to-all | bytes 1048576 | tf_op jit(solution)/shard_map/all_to_all | solution.py:64
  299.7 3.0 stack.13
  302.6 4.9 all-to-all-start.4
  308.1 14.9 %gather_fusion.3 = bf16[4096,128]{1,0:T(8,128)(2,1)} fusion(bf16[512,128]{1,0:T(8,128)(2,1)S(1)} %copy.96, s32[4096]{0:T(1024)S(1)} %fusion.94), kind=kCustom, calls=%fused_computation.3 | custom fusion | bytes 2113536 | tf_op jit(solution)/shard_map/gather | solution.py:158
  323.0 76.5 %all-to-all-done.4 = bf16[8,4,512,128]{3,2,1,0:T(8,128)(2,1)} async-done(((bf16[8,4,512,128]{3,2,1,0:T(8,128)(2,1)}), bf16[8,4,512,128]{3,2,1,0:T(8,128)(2,1)}, u32[]{:S(2)}, u32[]{:S(2)}) %all-to-all-start.4) | async-done | bytes 4194336 | tf_op jit(solution)/shard_map/all_to_all | solution.py:64
  399.5 4.6 copy.98
  404.1 17.0 %gather_fusion.4 = bf16[4096,128]{1,0:T(8,128)(2,1)} fusion(bf16[16384,128]{1,0:T(8,128)(2,1)} %bitcast.108, s32[4096]{0:T(1024)S(1)} %fusion.95), kind=kCustom, calls=%fused_computation.4 | custom fusion | bytes 2113536 | tf_op jit(solution)/shard_map/gather | solution.py:158
  421.1 3.3 fusion.124
  428.3 26.5 %scatter_custom_fusion.3 = f32[512,128]{1,0:T(8,128)S(1)} fusion(s32[4096]{0:T(1024)S(1)} %copy-done.7, f32[4096,128]{1,0:T(8,128)S(1)} %copy.99, f32[]{:T(128)} %constant.85.clone.1), kind=kCustom, calls=%fused_computation.71 | custom fusion | flops 524288 | bytes 262148 | tf_op jit(solution)/shard_map/scatter-add | solution.py:161
  456.5 9.3 %all_to_all.37 = bf16[4,1,512,128]{3,2,1,0:T(8,128)(2,1)S(1)} all-to-all(bf16[4,1,512,128]{3,2,1,0:T(8,128)(2,1)S(1)} %stack.14), channel_id=1, replica_groups=mesh['grp'=8,'dom_0'=4,'dom_1'=8] {'dom_0'}, dimensions={0} | all-to-all | bytes 1048576 | tf_op jit(solution)/shard_map/all_to_all | solution.py:64
  465.8 3.0 stack.15
  468.8 8.1 %all-to-all-start.6 = ((bf16[8,4,512,128]{3,2,1,0:T(8,128)(2,1)}), bf16[8,4,512,128]{3,2,1,0:T(8,128)(2,1)}, u32[]{:S(2)}, u32[]{:S(2)}) async-start(bf16[8,4,512,128]{3,2,1,0:T(8,128)(2,1)} %stack.15), calls=%async_computation.8 | async-start | bytes 8388608 | tf_op jit(solution)/shard_map/all_to_all | solution.py:64
  476.9 96.8 %all-to-all-done.6 = bf16[8,4,512,128]{3,2,1,0:T(8,128)(2,1)} async-done(((bf16[8,4,512,128]{3,2,1,0:T(8,128)(2,1)}), bf16[8,4,512,128]{3,2,1,0:T(8,128)(2,1)}, u32[]{:S(2)}, u32[]{:S(2)}) %all-to-all-start.6) | async-done | bytes 4194336 | tf_op jit(solution)/shard_map/all_to_all | solution.py:64
  573.8 4.6 copy.102
  578.4 4.3 gather_fusion.5
  (90 shorter events, 25.6 us)
Async XLA Ops:
  7.2 25.0 %copy-start = (bf16[1,768,128]{2,1,0:T(8,128)(2,1)S(1)}, bf16[1,768,128]{2,1,0:T(8,128)(2,1)}, u32[]{:S(2)}) copy-start(bf16[1,768,128]{2,1,0:T(8,128)(2,1)} %param.14) | copy-start | bytes 589828
  11.4 55.3 %all-to-all-start = ((bf16[32,24,128]{2,1,0:T(8,128)(2,1)}), bf16[32,24,128]{2,1,0:T(8,128)(2,1)S(1)}, u32[]{:S(2)}, u32[]{:S(2)}) async-start(bf16[32,24,128]{2,1,0:T(8,128)(2,1)} %bitcast.8), calls=%async_computation | async-start | bytes 393216 | tf_op jit(solution)/shard_map/all_to_all | solution.py:112
  23.2 170.7 %reduce-scatter.5.cloned.1.call-start = ((), (), s32[]{:S(2)}) async-start(), calls=%async_computation.10 | async-start | bytes 73728 | tf_op jit(solution)/shard_map/reduce_scatter | solution.py:143
  29.4 204.1 %reduce-scatter.3.cloned.1.call-start = ((), (), s32[]{:S(2)}) async-start(), calls=%async_computation.9 | async-start | bytes 4718592 | tf_op jit(solution)/shard_map/reduce_scatter | solution.py:140
  94.1 2.5 copy-start.8
  96.6 9.8 %copy-start.2 = (bf16[1,9216,128]{1,2,0:T(8,128)(2,1)S(1)}, bf16[1,9216,128]{1,2,0:T(8,128)(2,1)}, u32[]{:S(2)}) copy-start(bf16[1,9216,128]{1,2,0:T(8,128)(2,1)} %copy.81) | copy-start | bytes 7077892
  103.4 3.8 copy-start.1
  194.9 83.8 %copy-start.5 = (bf16[512,128]{1,0:T(8,128)(2,1)S(1)}, bf16[512,128]{1,0:T(8,128)(2,1)}, u32[]{:S(2)}) copy-start(bf16[512,128]{1,0:T(8,128)(2,1)} %param.21) | copy-start | bytes 393220
  266.7 21.4 %all-to-all-start.2 = ((f32[8,1,1,64,129]{4,3,2,1,0:T(8,128)}), f32[8,1,1,64,129]{4,3,2,1,0:T(8,128)S(1)}, u32[]{:S(2)}, u32[]{:S(2)}) async-start(f32[8,1,1,64,129]{4,3,2,1,0:T(8,128)} %broadcast_in_dim.24), calls=%async_computation.4 | async-start | bytes 1048576 | tf_op jit(solution)/shard_map/all_to_all | solution.py:41
  302.6 4.9 copy-start.3
  302.6 5.5 copy-start.6
  302.6 5.5 copy-start.7
  302.6 96.9 %all-to-all-start.4 = ((bf16[8,4,512,128]{3,2,1,0:T(8,128)(2,1)}), bf16[8,4,512,128]{3,2,1,0:T(8,128)(2,1)}, u32[]{:S(2)}, u32[]{:S(2)}) async-start(bf16[8,4,512,128]{3,2,1,0:T(8,128)(2,1)} %stack.13), calls=%async_computation.6 | async-start | bytes 8388608 | tf_op jit(solution)/shard_map/all_to_all | solution.py:64
  426.4 28.5 %copy-start.9 = (bf16[3,256,128]{2,1,0:T(8,128)(2,1)S(1)}, bf16[3,256,128]{2,1,0:T(8,128)(2,1)}, u32[]{:S(2)}) copy-start(bf16[3,256,128]{2,1,0:T(8,128)(2,1)} %param.26) | copy-start | bytes 589828
  456.4 12.4 %copy-start.4 = (bf16[512,128]{1,0:T(8,128)(2,1)}, bf16[512,128]{1,0:T(8,128)(2,1)S(1)}, u32[]{:S(2)}) copy-start(bf16[512,128]{1,0:T(8,128)(2,1)S(1)} %copy.101) | copy-start | bytes 393220
  468.8 105.0 %all-to-all-start.6 = ((bf16[8,4,512,128]{3,2,1,0:T(8,128)(2,1)}), bf16[8,4,512,128]{3,2,1,0:T(8,128)(2,1)}, u32[]{:S(2)}, u32[]{:S(2)}) async-start(bf16[8,4,512,128]{3,2,1,0:T(8,128)(2,1)} %stack.15), calls=%async_computation.8 | async-start | bytes 8388608 | tf_op jit(solution)/shard_map/all_to_all | solution.py:64
Sparse Core Ops, SparseCore 0:
  29.5 32.7 reduce-scatter.4
  194.0 39.5 reduce-scatter.2
